TPU v7x, 256 devices: a whole 4x4x8 slice. The times are simulated.
256 devices in a mesh: wide: 64 (over z, y, core), narrow: 4 (over x).
Axes of the slice: x: 4, y: 4, z: 8, core: 2. Of those that a mesh axis runs over, the one named last changes fastest.
Arguments:
- hidden_in: bfloat16 [1024, 4096], P('narrow', 'wide'), may hold values from -0.59765625 to 0.59765625
- cached_len: int32 [4], replicated, may hold values from 1 to 4096, 8192 in all
- k_cache: bfloat16 [4, 32768, 128], P('narrow', 'wide'), may hold values from -256 to 256
- v_cache: bfloat16 [4, 32768, 128], P('narrow', 'wide'), may hold values from -24 to 24
- attn_gain: bfloat16 [4096], replicated, may hold values from 0.099609375 to 1.8984375
- ffn_gain: bfloat16 [4096], replicated, may hold values from 0.099609375 to 1.8984375
- wqkv: bfloat16 [6144, 4096], P('wide', 'narrow'), may hold values from -0.09375 to 0.09375
- wo: bfloat16 [4096, 4096], P('wide', 'narrow'), may hold values from -0.09375 to 0.09375
- wgate: bfloat16 [14336, 4096], P('wide', 'narrow'), may hold values from -0.09375 to 0.09375
- wup: bfloat16 [14336, 4096], P('wide', 'narrow'), may hold values from -0.09375 to 0.09375
- wdown: bfloat16 [14336, 4096], P('wide', 'narrow'), may hold values from -0.125 to 0.125
Outputs:
- hidden_out: bfloat16 [1024, 4096], P('narrow', 'wide')
- new_k_cache: bfloat16 [4, 32768, 128], P('narrow', 'wide')
- new_v_cache: bfloat16 [4, 32768, 128], P('narrow', 'wide')
All inputs are finite; a program needn't handle non-finite values.
Results may differ from a plain program's by a relative error of at most 0.018.
The roundings to bfloat16 on the way count: a program that leaves them out, or rounds other values in their place, can miss the bound.
Values may be sent and summed in bfloat16 or wider, within the bound.
A program may use at most 64 MiB of HBM per device.

v0:
```python
import jax
import jax.numpy as jnp
from jax import lax
from jax.sharding import PartitionSpec as P

QH = 32
KVH = 8
HD = 128
WINDOW = 4096
NEG_FILL = -1e30


def partner(block, axis, stride):
    count = lax.axis_size(axis)
    route = []
    for low in range(count):
        high = low | 1 << stride
        if high != low and high < count:
            route += [(low, high), (high, low)]
    return lax.ppermute(block, axis, route)


def rms_scale(values, weights):
    widened = values.astype(jnp.float32)
    mean_square = jnp.mean(widened * widened, axis=-1, keepdims=True)
    return (widened * lax.rsqrt(mean_square + 1e-05) * weights.astype(jnp.float32)).astype(
        jnp.bfloat16
    )


def times_rows(left, right):
    return lax.dot_general(
        left, right, (((1,), (1,)), ((), ())), preferred_element_type=jnp.float32
    )


def rotate(heads, positions):
    half_width = heads.shape[-1] // 2
    exponent = jnp.arange(half_width, dtype=jnp.float32) * (2.0 / heads.shape[-1])
    frequency = jnp.power(10000.0, -exponent)
    angles = positions.astype(jnp.float32)[:, None] * frequency[None, :]
    cosine = jnp.cos(angles)[:, None, :]
    sine = jnp.sin(angles)[:, None, :]
    widened = heads.astype(jnp.float32)
    first_half = widened[..., :half_width]
    second_half = widened[..., half_width:]
    return jnp.concatenate(
        [first_half * cosine - second_half * sine, second_half * cosine + first_half * sine],
        axis=-1,
    ).astype(jnp.bfloat16)


def gather_cols(block):
    return lax.all_gather(block, "wide", axis=1, tiled=True)


def collect_heads(qkv_piece, sections):
    position = lax.axis_index("wide")
    for bit_index in range(sections):
        other_piece = partner(qkv_piece, "wide", bit_index)
        upper_half = position // 2**bit_index % 2 == 1
        qkv_piece = jnp.where(
            upper_half,
            jnp.concatenate([other_piece, qkv_piece], axis=1),
            jnp.concatenate([qkv_piece, other_piece], axis=1),
        )
    return qkv_piece


def combine(earlier, later):
    highest = jnp.maximum(earlier[0], later[0])
    left_scale = jnp.exp(earlier[0] - highest)
    right_scale = jnp.exp(later[0] - highest)
    return (
        highest,
        earlier[1] * left_scale + later[1] * right_scale,
        earlier[2] * left_scale[..., None] + later[2] * right_scale[..., None],
    )


def empty_state(row_count, group_size):
    return (
        jnp.full((row_count, group_size), NEG_FILL, jnp.float32),
        jnp.zeros((row_count, group_size), jnp.float32),
        jnp.zeros((row_count, group_size, HD), jnp.float32),
    )


def attend(queries, query_pos, keys, values, key_pos, key_live, soft_state):
    row_count, group_size, head_width = queries.shape
    flat_queries = queries.reshape(row_count * group_size, head_width)
    key_count = keys.shape[0]
    block_size = min(512, key_count)
    block_count = key_count // block_size
    lowest = jnp.min(query_pos)
    highest = jnp.max(query_pos)

    def key_step(carry, blocks):
        key_block, value_block, pos_block, live_block = blocks

        def score_block(running):
            peak_old, totals, accum = running
            scores = jnp.einsum(
                "qd,kd->qk", flat_queries, key_block, preferred_element_type=jnp.float32
            )
            scores = scores.reshape(row_count, group_size, block_size) * HD ** (-0.5)
            allowed = (
                live_block[None, :]
                & (pos_block[None, :] <= query_pos[:, None])
                & (pos_block[None, :] > query_pos[:, None] - WINDOW)
            )
            allowed = allowed[:, None, :]
            scores = jnp.where(allowed, scores, NEG_FILL)
            peak_new = jnp.maximum(peak_old, jnp.max(scores, axis=-1))
            factor = jnp.exp(peak_old - peak_new)
            exp_terms = jnp.where(allowed, jnp.exp(scores - peak_new[..., None]), 0.0)
            totals = totals * factor + jnp.sum(exp_terms, axis=-1)
            weights = exp_terms.astype(jnp.bfloat16).reshape(row_count * group_size, block_size)
            mixed = jnp.dot(weights, value_block, preferred_element_type=jnp.float32).reshape(
                row_count, group_size, head_width
            )
            return (peak_new, totals, accum * factor[..., None] + mixed)

        useful = jnp.any(live_block & (pos_block <= highest) & (pos_block > lowest - WINDOW))
        return (lax.cond(useful, score_block, lambda unchanged: unchanged, carry), None)

    blocks = (
        keys.reshape(block_count, block_size, head_width),
        values.reshape(block_count, block_size, head_width),
        key_pos.reshape(block_count, block_size),
        key_live.reshape(block_count, block_size),
    )
    soft_state, _ = lax.scan(key_step, soft_state, blocks)
    return soft_state


def per_device(
    hidden_in, cached_len, k_cache, v_cache, attn_gain, ffn_gain, wqkv, wo, wgate, wup, wdown
):
    qkv_full, out_full, gate_full, up_full, down_full = (
        lax.all_gather(wqkv, "narrow", axis=1, tiled=True),
        lax.all_gather(wo, "narrow", axis=1, tiled=True),
        lax.all_gather(wgate, "narrow", axis=1, tiled=True),
        lax.all_gather(wup, "narrow", axis=1, tiled=True),
        lax.all_gather(wdown, "narrow", axis=1, tiled=True),
    )
    wide_count = lax.axis_size("wide")
    part_count = wide_count // KVH
    sections = part_count.bit_length() - 1
    position = lax.axis_index("wide")
    part_index = position % part_count
    length = cached_len[lax.axis_index("narrow")]
    span_len = hidden_in.shape[0]
    group_size = QH // KVH
    steps_t = jnp.arange(span_len, dtype=jnp.int32)
    query_pos = length + steps_t
    normed_attn = rms_scale(gather_cols(hidden_in), attn_gain)
    qkv_piece = times_rows(normed_attn, qkv_full).astype(jnp.bfloat16)
    grouped = collect_heads(qkv_piece, sections)
    queries = rotate(grouped[:, : group_size * HD].reshape(span_len, group_size, HD), query_pos)
    new_keys = rotate(
        grouped[:, group_size * HD : (group_size + 1) * HD].reshape(span_len, 1, HD), query_pos
    ).reshape(span_len, HD)
    new_vals = grouped[:, (group_size + 1) * HD :]
    cache_keys = k_cache[0]
    cache_vals = v_cache[0]
    block_slots = cache_keys.shape[0]
    slot_pos = part_index * block_slots + jnp.arange(block_slots, dtype=jnp.int32)
    share_rows = span_len // part_count
    start_row = part_index * share_rows
    soft_state = empty_state(span_len, group_size)
    soft_state = attend(
        queries, query_pos, cache_keys, cache_vals, slot_pos, slot_pos < length, soft_state
    )
    soft_state = attend(
        queries,
        query_pos,
        lax.dynamic_slice_in_dim(new_keys, start_row, share_rows, 0),
        lax.dynamic_slice_in_dim(new_vals, start_row, share_rows, 0),
        lax.dynamic_slice_in_dim(query_pos, start_row, share_rows, 0),
        jnp.ones((share_rows,), jnp.bool_),
        soft_state,
    )
    for bit_index in range(sections):
        soft_state = combine(soft_state, partner(soft_state, "wide", bit_index))
    attended = (
        (soft_state[2] / soft_state[1][..., None])
        .astype(jnp.bfloat16)
        .reshape(span_len, group_size * HD)
    )
    width_share = group_size * HD // part_count
    own_cols = lax.dynamic_slice_in_dim(attended, part_index * width_share, width_share, 1)
    mixed_heads = gather_cols(own_cols)
    projected = times_rows(mixed_heads, out_full)
    after_attn = (hidden_in.astype(jnp.float32) + projected).astype(jnp.bfloat16)
    whole_after = gather_cols(after_attn)
    normed_ffn = rms_scale(whole_after, ffn_gain)
    gate_proj = times_rows(normed_ffn, gate_full)
    up_proj = times_rows(normed_ffn, up_full)
    activation = (jax.nn.silu(gate_proj) * up_proj).astype(jnp.bfloat16)
    summed = lax.psum_scatter(
        lax.dot_general(
            down_full, activation, (((0,), (1,)), ((), ())), preferred_element_type=jnp.float32
        ),
        "wide",
        scatter_dimension=0,
        tiled=True,
    )
    hidden_out = (after_attn.astype(jnp.float32) + summed.T).astype(jnp.bfloat16)
    offset = (slot_pos - length) % WINDOW
    fresh_slot = offset < span_len
    pick_row = jnp.minimum(offset, span_len - 1)
    new_k_cache = jnp.where(fresh_slot[:, None], jnp.take(new_keys, pick_row, axis=0), cache_keys)[
        None
    ]
    new_v_cache = jnp.where(fresh_slot[:, None], jnp.take(new_vals, pick_row, axis=0), cache_vals)[
        None
    ]
    return (hidden_out, new_k_cache, new_v_cache)


def solution(mesh):
    return jax.shard_map(
        per_device,
        mesh=mesh,
        in_specs=(
            P("narrow", "wide"),
            P(),
            P("narrow", "wide", None),
            P("narrow", "wide", None),
            P(),
            P(),
            P("wide", "narrow"),
            P("wide", "narrow"),
            P("wide", "narrow"),
            P("wide", "narrow"),
            P("wide", "narrow"),
        ),
        out_specs=(P("narrow", "wide"), P("narrow", "wide", None), P("narrow", "wide", None)),
        check_vma=False,
    )
```

profile of v0, /device:TPU:2, one launch (start us, length us, event | category | flops | bytes accessed | tf_op | source)
XLA Modules:
  0.0 569.9 jit_solution(13301387686112721194)
XLA Ops:
  13.1 2.0 fusion.58
  15.7 14.4 %all_gather.25 = bf16[96,4096]{1,0:T(8,128)(2,1)S(1)} all-gather(bf16[96,1024]{1,0:T(8,128)(2,1)} %param.23), channel_id=1, replica_groups=mesh['wide'=64,'narrow'=4] {'narrow'}, dimensions={1}, use_global_device_ids=true | all-gather | bytes 983040 | tf_op jit(solution)/shard_map/all_gather | solution.py:141
  30.1 61.0 %all-gather.7.cloned.1.call-done = bf16[256,4096]{0,1:T(8,128)(2,1)} async-done(((bf16[256,64]{0,1:T(8,128)(2,1)}), bf16[256,4096]{0,1:T(8,128)(2,1)}) %all-gather.7.cloned.1.call-update) | async-done | bytes 2097168 | tf_op jit(solution)/shard_map/all_gather | solution.py:54
  91.0 2.3 fusion.16
  94.6 1.9 and_reduce_fusion
  99.2 4.4 collective-permute-done.1
  103.6 2.2 collective-permute-start.2
  106.1 5.3 collective-permute-done.2
  113.9 11.8 %conditional.2 = ((f32[256,4]{1,0:T(8,128)S(1)}, f32[256,4]{1,0:T(8,128)}, f32[256,4,128]{2,0,1:T(8,128)S(1)})) conditional(s32[]{:T(128)} %convert_element_type.91, (f32[256,4]{1,0:T(8,128)S(1)}, f32[256,4]{1,0:T(8,128)}, f32[256,4,128]{2,0,1:T(8,128)S(1)}) %tuple.31, (pred[512]{0:T(512)(128)(4,1)S(1)}, s32[512]{0:T(512)S(1)}, s32[256]{0:T(256)S(1)}, ...), branch_computations={%region_5.6_spmd, %region_6.9_spmd} | conditional | flops 273942784 | bytes 13486680 | solution.py:125
  115.1 1.5 fusion
  117.4 1.6 max.12
  120.0 1.8 fusion.1
  122.0 1.7 multiply_add_fusion
  123.7 1.4 dot_general.9
  125.7 4.8 conditional.3
  133.2 1.5 collective-permute-start.10
  135.2 11.6 %collective-permute-done.10 = f32[256,4]{0,1:T(4,128)S(1)} collective-permute-done((f32[256,4]{0,1:T(4,128)S(1)}, f32[256,4]{0,1:T(4,128)S(1)}, u32[]{:S(2)}, u32[]{:S(2)}) %collective-permute-start.10) | collective-permute-done | bytes 4128 | tf_op jit(solution)/shard_map/ppermute | solution.py:20
  147.1 3.5 collective-permute-start.11
  150.7 11.1 %collective-permute-done.11 = f32[256,4]{0,1:T(4,128)S(1)} collective-permute-done((f32[256,4]{0,1:T(4,128)S(1)}, f32[256,4]{0,1:T(4,128)S(1)}, u32[]{:S(2)}, u32[]{:S(2)}) %collective-permute-start.11) | collective-permute-done | bytes 4128 | tf_op jit(solution)/shard_map/ppermute | solution.py:20
  162.7 12.8 %all_gather.27 = bf16[64,4096]{1,0:T(8,128)(2,1)S(1)} all-gather(bf16[64,1024]{1,0:T(8,128)(2,1)S(1)} %copy-done.14), channel_id=1, replica_groups=mesh['wide'=64,'narrow'=4] {'narrow'}, dimensions={1}, use_global_device_ids=true | all-gather | bytes 655360 | tf_op jit(solution)/shard_map/all_gather | solution.py:142
  175.5 61.0 %all-gather.9.cloned.1.call-done = bf16[256,4096]{0,1:T(8,128)(2,1)} async-done(((bf16[256,64]{0,1:T(8,128)(2,1)}), bf16[256,4096]{0,1:T(8,128)(2,1)}) %all-gather.9.cloned.1.call-update) | async-done | bytes 2097168 | tf_op jit(solution)/shard_map/all_gather | solution.py:54
  236.4 2.7 fusion.30
  240.9 73.8 %all-gather.11.cloned.1.call-done = bf16[256,4096]{0,1:T(8,128)(2,1)} async-done(((bf16[256,64]{0,1:T(8,128)(2,1)}), bf16[256,4096]{0,1:T(8,128)(2,1)}) %all-gather.11.cloned.1.call-update) | async-done | bytes 2097168 | tf_op jit(solution)/shard_map/all_gather | solution.py:54
  314.8 2.3 fusion.19
  317.1 27.2 %all-gather.13.cloned.1.call-done = bf16[224,4096]{1,0:T(8,128)(2,1)} async-done(((bf16[224,1024]{1,0:T(8,128)(2,1)}), bf16[224,4096]{1,0:T(8,128)(2,1)}) %all-gather.13.cloned.1.call-update) | async-done | bytes 1835024 | tf_op jit(solution)/shard_map/all_gather | solution.py:143
  344.4 2.3 fusion.31
  346.7 30.5 %all-gather.15.cloned.1.call-done = bf16[224,4096]{1,0:T(8,128)(2,1)} async-done(((bf16[224,1024]{1,0:T(8,128)(2,1)}), bf16[224,4096]{1,0:T(8,128)(2,1)}) %all-gather.15.cloned.1.call-update) | async-done | bytes 1835024 | tf_op jit(solution)/shard_map/all_gather | solution.py:144
  377.3 32.9 %all-gather.17.cloned.1.call-done = bf16[224,4096]{1,0:T(8,128)(2,1)} async-done(((bf16[224,1024]{1,0:T(8,128)(2,1)}), bf16[224,4096]{1,0:T(8,128)(2,1)}) %all-gather.17.cloned.1.call-update) | async-done | bytes 1835024 | tf_op jit(solution)/shard_map/all_gather | solution.py:145
  410.2 6.4 %convolution_bitcast_fusion = f32[4096,256]{1,0:T(8,128)} fusion(bf16[224,4096]{1,0:T(8,128)(2,1)} %all-gather.17.cloned.1.call-done, bf16[224,4096]{1,0:T(8,128)(2,1)} %all-gather.15.cloned.1.call-done, bf16[256,4096]{0,1:T(8,128)(2,1)S(1)} %copy-done, f32[4096]{0:T(1024)S(1)} %convert_element_type.105, f32[256]{0:T(256)S(1)} %add_rsqrt_fusion, ...), kind=kOutput, calls=%fused_computation.32 | convolution fusion | flops 944062464 | bytes 10208256 | tf_op jit(solution)/shard_map/dot_general | solution.py:202
  418.2 1.3 gather_fusion
  421.9 139.7 %reduce-scatter.2.cloned.1.call-done = f32[64,256]{1,0:T(8,128)} async-done(((f32[4096,256]{1,0:T(8,128)}), f32[64,256]{1,0:T(8,128)}) %reduce-scatter.2.cloned.1.call-update) | async-done | bytes 65552 | tf_op jit(solution)/shard_map/reduce_scatter | solution.py:201
  561.6 1.5 fusion.52
  (135 shorter events, 29.5 us)
Async XLA Ops:
  7.2 83.9 %all-gather.7.cloned.1.call-start = ((), (), s32[]{:S(2)}) async-start(), calls=%async_computation.1 | async-start | bytes 2129920 | tf_op jit(solution)/shard_map/all_gather | solution.py:54
  7.9 228.5 %all-gather.9.cloned.1.call-start = ((), (), s32[]{:S(2)}) async-start(), calls=%async_computation.2 | async-start | bytes 2129920 | tf_op jit(solution)/shard_map/all_gather | solution.py:54
  91.0 2.3 copy-start.1
  94.2 4.3 collective-permute-start
  98.5 5.0 collective-permute-start.1
  103.6 7.8 %collective-permute-start.2 = (bf16[256,384]{0,1:T(8,128)(2,1)S(1)}, bf16[256,384]{0,1:T(8,128)(2,1)S(1)}, u32[]{:S(2)}, u32[]{:S(2)}) collective-permute-start(bf16[256,384]{0,1:T(8,128)(2,1)S(1)} %maximum_select_fusion.1), channel_id=1, source_target_pairs={{0,16},{16,0},{4,20},{20,4},{8,24},{24,8},{12,28},{28,12},{32,48},... | collective-permute-start | bytes 589832 | tf_op jit(solution)/shard_map/ppermute | solution.py:20
  121.8 3.3 copy-start.7
  123.7 2.0 copy-start.2
  125.7 4.1 copy-start.4
  130.5 2.0 collective-permute-start.4
  130.6 1.9 collective-permute-start.3
  131.1 1.4 collective-permute-start.9
  132.5 30.2 %copy-start.14 = (bf16[64,1024]{1,0:T(8,128)(2,1)S(1)}, bf16[64,1024]{1,0:T(8,128)(2,1)}, u32[]{:S(2)}) copy-start(bf16[64,1024]{1,0:T(8,128)(2,1)} %param.24) | copy-start | bytes 393220
  132.6 103.8 %copy-start.13 = (bf16[256,64]{0,1:T(8,128)(2,1)S(1)}, bf16[256,64]{0,1:T(8,128)(2,1)}, u32[]{:S(2)}) copy-start(bf16[256,64]{0,1:T(8,128)(2,1)} %param.17) | copy-start | bytes 98308
  132.6 14.2 %collective-permute-start.6 = (f32[256,4,128]{0,2,1:T(8,128)S(1)}, f32[256,4,128]{0,2,1:T(8,128)S(1)}, u32[]{:S(2)}, u32[]{:S(2)}) collective-permute-start(f32[256,4,128]{0,2,1:T(8,128)S(1)} %multiply_add_fusion.3), channel_id=1, source_target_pairs={{0,8},{8,0},{4,12},{12,4},{16,24},{24,16},{20,28},{28,20},{32,40},... | collective-permute-start | bytes 1572872 | tf_op jit(solution)/shard_map/ppermute | solution.py:20
  133.2 13.6 %collective-permute-start.10 = (f32[256,4]{0,1:T(4,128)S(1)}, f32[256,4]{0,1:T(4,128)S(1)}, u32[]{:S(2)}, u32[]{:S(2)}) collective-permute-start(f32[256,4]{0,1:T(4,128)S(1)} %get-tuple-element.243), channel_id=1, source_target_pairs={{0,8},{8,0},{4,12},{12,4},{16,24},{24,16},{20,28},{28,20},{32,40},... | collective-permute-start | bytes 12296 | tf_op jit(solution)/shard_map/ppermute | solution.py:20
  134.7 12.1 %collective-permute-start.5 = (f32[256,4]{0,1:T(4,128)S(1)}, f32[256,4]{0,1:T(4,128)S(1)}, u32[]{:S(2)}, u32[]{:S(2)}) collective-permute-start(f32[256,4]{0,1:T(4,128)S(1)} %get-tuple-element.246), channel_id=1, source_target_pairs={{0,8},{8,0},{4,12},{12,4},{16,24},{24,16},{20,28},{28,20},{32,40},... | collective-permute-start | bytes 12296 | tf_op jit(solution)/shard_map/ppermute | solution.py:20
  147.0 14.9 %collective-permute-start.8 = (f32[256,4,128]{0,2,1:T(8,128)S(1)}, f32[256,4,128]{0,2,1:T(8,128)S(1)}, u32[]{:S(2)}, u32[]{:S(2)}) collective-permute-start(f32[256,4,128]{0,2,1:T(8,128)S(1)} %multiply_add_fusion.2), channel_id=1, source_target_pairs={{0,16},{16,0},{4,20},{20,4},{8,24},{24,8},{12,28},{28,12},{32,48},... | collective-permute-start | bytes 1572872 | tf_op jit(solution)/shard_map/ppermute | solution.py:20
  147.1 14.8 %collective-permute-start.11 = (f32[256,4]{0,1:T(4,128)S(1)}, f32[256,4]{0,1:T(4,128)S(1)}, u32[]{:S(2)}, u32[]{:S(2)}) collective-permute-start(f32[256,4]{0,1:T(4,128)S(1)} %get-tuple-element.239), channel_id=1, source_target_pairs={{0,16},{16,0},{4,20},{20,4},{8,24},{24,8},{12,28},{28,12},{32,48},... | collective-permute-start | bytes 12296 | tf_op jit(solution)/shard_map/ppermute | solution.py:20
  150.6 11.3 %collective-permute-start.7 = (f32[256,4]{0,1:T(4,128)S(1)}, f32[256,4]{0,1:T(4,128)S(1)}, u32[]{:S(2)}, u32[]{:S(2)}) collective-permute-start(f32[256,4]{0,1:T(4,128)S(1)} %get-tuple-element.242), channel_id=1, source_target_pairs={{0,16},{16,0},{4,20},{20,4},{8,24},{24,8},{12,28},{28,12},{32,48},... | collective-permute-start | bytes 12296 | tf_op jit(solution)/shard_map/ppermute | solution.py:20
  162.6 152.1 %all-gather.11.cloned.1.call-start = ((), (), s32[]{:S(2)}) async-start(), calls=%async_computation.3 | async-start | bytes 2129920 | tf_op jit(solution)/shard_map/all_gather | solution.py:54
  175.5 65.5 %copy-start.15 = (bf16[4096]{0:T(1024)(128)(2,1)S(1)}, bf16[4096]{0:T(1024)(128)(2,1)}, u32[]{:S(2)}) copy-start(bf16[4096]{0:T(1024)(128)(2,1)} %param.22) | copy-start | bytes 24580
  239.1 105.2 %all-gather.13.cloned.1.call-start = ((), (), s32[]{:S(2)}) async-start(), calls=%async_computation.4 | async-start | bytes 2293760 | tf_op jit(solution)/shard_map/all_gather | solution.py:143
  239.7 137.5 %all-gather.15.cloned.1.call-start = ((), (), s32[]{:S(2)}) async-start(), calls=%async_computation.5 | async-start | bytes 2293760 | tf_op jit(solution)/shard_map/all_gather | solution.py:144
  240.3 169.9 %all-gather.17.cloned.1.call-start = ((), (), s32[]{:S(2)}) async-start(), calls=%async_computation.6 | async-start | bytes 2293760 | tf_op jit(solution)/shard_map/all_gather | solution.py:145
  240.9 320.7 %reduce-scatter.2.cloned.1.call-start = ((), (), s32[]{:S(2)}) async-start(), calls=%async_computation.7 | async-start | bytes 4259840 | tf_op jit(solution)/shard_map/reduce_scatter | solution.py:201
  314.8 29.6 %copy-start = (bf16[256,4096]{0,1:T(8,128)(2,1)S(1)}, bf16[256,4096]{0,1:T(8,128)(2,1)}, u32[]{:S(2)}) copy-start(bf16[256,4096]{0,1:T(8,128)(2,1)} %all-gather.11.cloned.1.call-done) | copy-start | bytes 6291460
  416.5 1.6 copy-start.10
  416.5 1.6 copy-start.12
  416.6 4.4 copy-start.5
  416.6 4.4 copy-start.6
  416.6 145.0 %copy-start.8 = (bf16[256,64]{0,1:T(8,128)(2,1)S(1)}, bf16[256,64]{0,1:T(8,128)(2,1)}, u32[]{:S(2)}) copy-start(bf16[256,64]{0,1:T(8,128)(2,1)} %fusion.30) | copy-start | bytes 98308
  (3 other events, 4.0 us)
Sparse Core Ops, SparseCore 0:
  10.8 80.2 all-gather.6
  162.8 73.6 all-gather.8
  239.8 74.9 all-gather.10
  316.4 27.8 all-gather.12
  346.0 31.1 all-gather.14
  378.9 31.1 all-gather.16
  416.7 144.8 reduce-scatter.1
where the time goes:
time: 570 us
  waiting for transfers between devices  462 us (81%)
  blocking collectives  27.1 us (5%)
  other arithmetic  25.7 us (5%)
  between operations  16.5 us (3%)
  matrix products  14.7 us (3%)
  local copies, waits for them, and re-layouts  12.8 us (2%)
  starting transfers between devices  10.4 us (2%)
    all_gather x3, waiting for transfers between devices, gather_cols(): return lax.all_gather(block, 'wide', axis=1, tiled=True)  196 us
    reduce_scatter x1, waiting for transfers between devices, per_device(): lax.psum_scatter(lax.dot_general(down_full, activation, (((0,), (1,)), ((...  140 us
    ppermute x12, waiting for transfers between devices, partner(): return lax.ppermute(block, axis, route)  33.9 us
    all_gather x1, waiting for transfers between devices, per_device(): lax.all_gather(wdown, 'narrow', axis=1, tiled=True)  32.9 us
    all_gather x1, waiting for transfers between devices, per_device(): lax.all_gather(wup, 'narrow', axis=1, tiled=True)  30.5 us
    all_gather x1, waiting for transfers between devices, per_device(): lax.all_gather(wgate, 'narrow', axis=1, tiled=True)  27.2 us
    all_gather x1, blocking collectives, per_device(): lax.all_gather(wqkv, 'narrow', axis=1, tiled=True)  14.4 us
    all_gather x1, blocking collectives, per_device(): lax.all_gather(wo, 'narrow', axis=1, tiled=True)  12.8 us
  transfers between devices with their start and end apart: 19, of which 12 were waited for; matrix products, arithmetic and copies ran while one was open for 3% of the time, Pallas kernels for 0%

commit v1 on v0

--- a/solution.py
+++ b/solution.py
@@ -142,7 +142,9 @@
         lax.all_gather(wo, "narrow", axis=1, tiled=True),
         lax.all_gather(wgate, "narrow", axis=1, tiled=True),
         lax.all_gather(wup, "narrow", axis=1, tiled=True),
-        lax.all_gather(wdown, "narrow", axis=1, tiled=True),
+        jnp.concatenate(
+            lax.all_to_all(jnp.stack([wdown] * lax.axis_size("narrow")), "narrow", 0, 0), axis=1
+        ),
     )
     wide_count = lax.axis_size("wide")
     part_count = wide_count // KVH

time: 570 us -> 539 us (0.946)
  waiting for transfers between devices: 462 us -> 422 us
    all_gather x1 -> x0, waiting for transfers between devices: 32.9 us -> none  [per_device(): lax.all_gather(wdown, 'narrow', axis=1, tiled=True)]
    all_gather x3, waiting for transfers between devices: 196 us -> 166 us  [gather_cols(): return lax.all_gather(block, 'wide', axis=1, tiled=True)]
    all_to_all x0 -> x1, waiting for transfers between devices: none -> 22.5 us  [per_device(): lax.all_to_all(jnp.stack([wdown] * lax.axis_size('narrow')), 'narrow', 0, 0)]
  transfers between devices with their start and end apart: 19 -> 19, of which waited for: 12 -> 12; matrix products, arithmetic and copies ran while one was open for 3% -> 4% of each run, Pallas kernels for 0% -> 0%
where the time goes in v1:
time: 539 us; the launch traced here: 538 us
  waiting for transfers between devices  422 us (78%)
  blocking collectives  27.3 us (5%)
  other arithmetic  25.2 us (5%)
  local copies, waits for them, and re-layouts  16.6 us (3%)
  between operations  16.5 us (3%)
  starting transfers between devices  15.4 us (3%)
  matrix products  14.7 us (3%)
    all_gather x3, waiting for transfers between devices, gather_cols(): return lax.all_gather(block, 'wide', axis=1, tiled=True)  166 us
    reduce_scatter x1, waiting for transfers between devices, per_device(): lax.psum_scatter(lax.dot_general(down_full, activation, (((0,), (1,)), ((...  140 us
    ppermute x12, waiting for transfers between devices, partner(): return lax.ppermute(block, axis, route)  33.8 us
    all_gather x1, waiting for transfers between devices, per_device(): lax.all_gather(wup, 'narrow', axis=1, tiled=True)  30.5 us
    all_gather x1, waiting for transfers between devices, per_device(): lax.all_gather(wgate, 'narrow', axis=1, tiled=True)  27.2 us
    all_to_all x1, waiting for transfers between devices, per_device(): lax.all_to_all(jnp.stack([wdown] * lax.axis_size('narrow')), 'narrow', 0, 0)  22.5 us
    all_gather x1, blocking collectives, per_device(): lax.all_gather(wqkv, 'narrow', axis=1, tiled=True)  14.4 us
    all_gather x1, blocking collectives, per_device(): lax.all_gather(wo, 'narrow', axis=1, tiled=True)  12.9 us
  transfers between devices with their start and end apart: 19, of which 12 were waited for; matrix products, arithmetic and copies ran while one was open for 4% of the time, Pallas kernels for 0%

profile of v1, /device:TPU:2, one launch (start us, length us, event | category | flops | bytes accessed | tf_op | source)
XLA Modules:
  0.0 538.0 jit_solution(15047786613520731180)
XLA Ops:
  12.9 1.9 fusion.58
  15.4 14.4 %all_gather.22 = bf16[96,4096]{1,0:T(8,128)(2,1)S(1)} all-gather(bf16[96,1024]{1,0:T(8,128)(2,1)} %param.23), channel_id=1, replica_groups=mesh['wide'=64,'narrow'=4] {'narrow'}, dimensions={1}, use_global_device_ids=true | all-gather | bytes 983040 | tf_op jit(solution)/shard_map/all_gather | solution.py:141
  29.8 61.3 %all-gather.6.cloned.1.call-done = bf16[256,4096]{0,1:T(8,128)(2,1)} async-done(((bf16[256,64]{0,1:T(8,128)(2,1)}), bf16[256,4096]{0,1:T(8,128)(2,1)}) %all-gather.6.cloned.1.call-update) | async-done | bytes 2097168 | tf_op jit(solution)/shard_map/all_gather | solution.py:54
  91.0 2.3 fusion.16
  94.6 1.8 and_reduce_fusion
  99.1 4.4 collective-permute-done.1
  103.6 2.2 collective-permute-start.2
  106.1 5.3 collective-permute-done.2
  113.9 12.6 %conditional.2 = ((f32[256,4]{1,0:T(8,128)S(1)}, f32[256,4]{1,0:T(8,128)}, f32[256,4,128]{2,0,1:T(8,128)S(1)})) conditional(s32[]{:T(128)} %convert_element_type.91, (f32[256,4]{1,0:T(8,128)S(1)}, f32[256,4]{1,0:T(8,128)}, f32[256,4,128]{2,0,1:T(8,128)S(1)}) %tuple.31, (pred[512]{0:T(512)(128)(4,1)S(1)}, s32[512]{0:T(512)S(1)}, s32[256]{0:T(256)S(1)}, ...), branch_computations={%region_5.6_spmd, %region_6.9_spmd} | conditional | flops 273942784 | bytes 13470268 | solution.py:125
  115.1 1.5 fusion
  117.4 1.6 max.12
  120.0 1.8 fusion.1
  121.9 1.7 multiply_add_fusion
  126.5 4.8 conditional.3
  134.1 1.5 collective-permute-start.10
  136.2 11.6 %collective-permute-done.10 = f32[256,4]{0,1:T(4,128)S(1)} collective-permute-done((f32[256,4]{0,1:T(4,128)S(1)}, f32[256,4]{0,1:T(4,128)S(1)}, u32[]{:S(2)}, u32[]{:S(2)}) %collective-permute-start.10) | collective-permute-done | bytes 4128 | tf_op jit(solution)/shard_map/ppermute | solution.py:20
  148.0 3.5 collective-permute-start.11
  151.6 11.1 %collective-permute-done.11 = f32[256,4]{0,1:T(4,128)S(1)} collective-permute-done((f32[256,4]{0,1:T(4,128)S(1)}, f32[256,4]{0,1:T(4,128)S(1)}, u32[]{:S(2)}, u32[]{:S(2)}) %collective-permute-start.11) | collective-permute-done | bytes 4128 | tf_op jit(solution)/shard_map/ppermute | solution.py:20
  163.6 12.9 %all_gather.24 = bf16[64,4096]{1,0:T(8,128)(2,1)S(1)} all-gather(bf16[64,1024]{1,0:T(8,128)(2,1)S(1)} %copy-done.14), channel_id=1, replica_groups=mesh['wide'=64,'narrow'=4] {'narrow'}, dimensions={1}, use_global_device_ids=true | all-gather | bytes 655360 | tf_op jit(solution)/shard_map/all_gather | solution.py:142
  176.5 60.8 %all-gather.8.cloned.1.call-done = bf16[256,4096]{0,1:T(8,128)(2,1)} async-done(((bf16[256,64]{0,1:T(8,128)(2,1)}), bf16[256,4096]{0,1:T(8,128)(2,1)}) %all-gather.8.cloned.1.call-update) | async-done | bytes 2097168 | tf_op jit(solution)/shard_map/all_gather | solution.py:54
  237.4 2.7 fusion.30
  241.2 1.5 stack.2
  242.7 4.9 all-to-all-start
  247.7 22.5 %all-to-all-done = bf16[4,224,1024]{2,1,0:T(8,128)(2,1)S(1)} async-done(((bf16[4,224,1024]{2,1,0:T(8,128)(2,1)}), bf16[4,224,1024]{2,1,0:T(8,128)(2,1)S(1)}, u32[]{:S(2)}, u32[]{:S(2)}) %all-to-all-start) | async-done | bytes 1835040 | tf_op jit(solution)/shard_map/all_to_all | solution.py:146
  271.6 44.1 %all-gather.10.cloned.1.call-done = bf16[256,4096]{0,1:T(8,128)(2,1)} async-done(((bf16[256,64]{0,1:T(8,128)(2,1)}), bf16[256,4096]{0,1:T(8,128)(2,1)}) %all-gather.10.cloned.1.call-update) | async-done | bytes 2097168 | tf_op jit(solution)/shard_map/all_gather | solution.py:54
  315.7 2.3 fusion.19
  318.0 27.2 %all-gather.12.cloned.1.call-done = bf16[224,4096]{1,0:T(8,128)(2,1)} async-done(((bf16[224,1024]{1,0:T(8,128)(2,1)}), bf16[224,4096]{1,0:T(8,128)(2,1)}) %all-gather.12.cloned.1.call-update) | async-done | bytes 1835024 | tf_op jit(solution)/shard_map/all_gather | solution.py:143
  345.3 2.3 fusion.31
  347.6 30.5 %all-gather.14.cloned.1.call-done = bf16[224,4096]{1,0:T(8,128)(2,1)} async-done(((bf16[224,1024]{1,0:T(8,128)(2,1)}), bf16[224,4096]{1,0:T(8,128)(2,1)}) %all-gather.14.cloned.1.call-update) | async-done | bytes 1835024 | tf_op jit(solution)/shard_map/all_gather | solution.py:144
  378.2 6.4 %convolution_bitcast_fusion = f32[4096,256]{1,0:T(8,128)} fusion(bf16[224,4096]{1,0:T(8,128)(2,1)} %bitcast.57, bf16[224,4096]{1,0:T(8,128)(2,1)} %all-gather.14.cloned.1.call-done, bf16[256,4096]{0,1:T(8,128)(2,1)S(1)} %copy-done, f32[4096]{0:T(1024)S(1)} %convert_element_type.105, f32[256]{0:T(256)S(1)} %add_rsqrt_fusion, f32[256,224]{0,1:T(8,128)S(1)} %fusion.31), kind=kOutput, calls=%fused_computation.32 | convolution fusion | flops 944062464 | bytes 10208256 | tf_op jit(solution)/shard_map/dot_general | solution.py:204
  389.7 139.9 %reduce-scatter.2.cloned.1.call-done = f32[64,256]{1,0:T(8,128)} async-done(((f32[4096,256]{1,0:T(8,128)}), f32[64,256]{1,0:T(8,128)}) %reduce-scatter.2.cloned.1.call-update) | async-done | bytes 65552 | tf_op jit(solution)/shard_map/reduce_scatter | solution.py:203
  529.7 1.5 fusion.52
  (136 shorter events, 33.8 us)
Async XLA Ops:
  7.2 83.9 %all-gather.6.cloned.1.call-start = ((), (), s32[]{:S(2)}) async-start(), calls=%async_computation.2 | async-start | bytes 2129920 | tf_op jit(solution)/shard_map/all_gather | solution.py:54
  7.9 229.5 %all-gather.8.cloned.1.call-start = ((), (), s32[]{:S(2)}) async-start(), calls=%async_computation.3 | async-start | bytes 2129920 | tf_op jit(solution)/shard_map/all_gather | solution.py:54
  91.0 2.3 copy-start.1
  94.2 4.3 collective-permute-start
  98.5 5.0 collective-permute-start.1
  103.6 7.8 %collective-permute-start.2 = (bf16[256,384]{0,1:T(8,128)(2,1)S(1)}, bf16[256,384]{0,1:T(8,128)(2,1)S(1)}, u32[]{:S(2)}, u32[]{:S(2)}) collective-permute-start(bf16[256,384]{0,1:T(8,128)(2,1)S(1)} %maximum_select_fusion.1), channel_id=1, source_target_pairs={{0,16},{16,0},{4,20},{20,4},{8,24},{24,8},{12,28},{28,12},{32,48},... | collective-permute-start | bytes 589832 | tf_op jit(solution)/shard_map/ppermute | solution.py:20
  121.8 4.1 copy-start.6
  126.5 4.0 copy-start.3
  131.3 2.0 collective-permute-start.4
  131.3 1.9 collective-permute-start.9
  131.8 1.4 collective-permute-start.3
  133.3 30.3 %copy-start.14 = (bf16[64,1024]{1,0:T(8,128)(2,1)S(1)}, bf16[64,1024]{1,0:T(8,128)(2,1)}, u32[]{:S(2)}) copy-start(bf16[64,1024]{1,0:T(8,128)(2,1)} %param.24) | copy-start | bytes 393220
  133.3 104.0 %copy-start.13 = (bf16[256,64]{0,1:T(8,128)(2,1)S(1)}, bf16[256,64]{0,1:T(8,128)(2,1)}, u32[]{:S(2)}) copy-start(bf16[256,64]{0,1:T(8,128)(2,1)} %param.17) | copy-start | bytes 98308
  133.4 14.4 %collective-permute-start.6 = (f32[256,4,128]{0,2,1:T(8,128)S(1)}, f32[256,4,128]{0,2,1:T(8,128)S(1)}, u32[]{:S(2)}, u32[]{:S(2)}) collective-permute-start(f32[256,4,128]{0,2,1:T(8,128)S(1)} %multiply_add_fusion.3), channel_id=1, source_target_pairs={{0,8},{8,0},{4,12},{12,4},{16,24},{24,16},{20,28},{28,20},{32,40},... | collective-permute-start | bytes 1572872 | tf_op jit(solution)/shard_map/ppermute | solution.py:20
  134.1 13.6 %collective-permute-start.10 = (f32[256,4]{0,1:T(4,128)S(1)}, f32[256,4]{0,1:T(4,128)S(1)}, u32[]{:S(2)}, u32[]{:S(2)}) collective-permute-start(f32[256,4]{0,1:T(4,128)S(1)} %get-tuple-element.252), channel_id=1, source_target_pairs={{0,8},{8,0},{4,12},{12,4},{16,24},{24,16},{20,28},{28,20},{32,40},... | collective-permute-start | bytes 12296 | tf_op jit(solution)/shard_map/ppermute | solution.py:20
  135.7 12.1 %collective-permute-start.5 = (f32[256,4]{0,1:T(4,128)S(1)}, f32[256,4]{0,1:T(4,128)S(1)}, u32[]{:S(2)}, u32[]{:S(2)}) collective-permute-start(f32[256,4]{0,1:T(4,128)S(1)} %get-tuple-element.255), channel_id=1, source_target_pairs={{0,8},{8,0},{4,12},{12,4},{16,24},{24,16},{20,28},{28,20},{32,40},... | collective-permute-start | bytes 12296 | tf_op jit(solution)/shard_map/ppermute | solution.py:20
  147.9 14.9 %collective-permute-start.8 = (f32[256,4,128]{0,2,1:T(8,128)S(1)}, f32[256,4,128]{0,2,1:T(8,128)S(1)}, u32[]{:S(2)}, u32[]{:S(2)}) collective-permute-start(f32[256,4,128]{0,2,1:T(8,128)S(1)} %multiply_add_fusion.2), channel_id=1, source_target_pairs={{0,16},{16,0},{4,20},{20,4},{8,24},{24,8},{12,28},{28,12},{32,48},... | collective-permute-start | bytes 1572872 | tf_op jit(solution)/shard_map/ppermute | solution.py:20
  148.0 14.7 %collective-permute-start.11 = (f32[256,4]{0,1:T(4,128)S(1)}, f32[256,4]{0,1:T(4,128)S(1)}, u32[]{:S(2)}, u32[]{:S(2)}) collective-permute-start(f32[256,4]{0,1:T(4,128)S(1)} %get-tuple-element.248), channel_id=1, source_target_pairs={{0,16},{16,0},{4,20},{20,4},{8,24},{24,8},{12,28},{28,12},{32,48},... | collective-permute-start | bytes 12296 | tf_op jit(solution)/shard_map/ppermute | solution.py:20
  151.5 11.3 %collective-permute-start.7 = (f32[256,4]{0,1:T(4,128)S(1)}, f32[256,4]{0,1:T(4,128)S(1)}, u32[]{:S(2)}, u32[]{:S(2)}) collective-permute-start(f32[256,4]{0,1:T(4,128)S(1)} %get-tuple-element.251), channel_id=1, source_target_pairs={{0,16},{16,0},{4,20},{20,4},{8,24},{24,8},{12,28},{28,12},{32,48},... | collective-permute-start | bytes 12296 | tf_op jit(solution)/shard_map/ppermute | solution.py:20
  163.5 77.7 %copy-start.7 = (bf16[224,1024]{1,0:T(8,128)(2,1)S(1)}, bf16[224,1024]{1,0:T(8,128)(2,1)}, u32[]{:S(2)}) copy-start(bf16[224,1024]{1,0:T(8,128)(2,1)} %param.27) | copy-start | bytes 1376260
  163.5 152.1 %all-gather.10.cloned.1.call-start = ((), (), s32[]{:S(2)}) async-start(), calls=%async_computation.4 | async-start | bytes 2129920 | tf_op jit(solution)/shard_map/all_gather | solution.py:54
  240.0 105.2 %all-gather.12.cloned.1.call-start = ((), (), s32[]{:S(2)}) async-start(), calls=%async_computation.5 | async-start | bytes 2293760 | tf_op jit(solution)/shard_map/all_gather | solution.py:143
  240.6 137.5 %all-gather.14.cloned.1.call-start = ((), (), s32[]{:S(2)}) async-start(), calls=%async_computation.6 | async-start | bytes 2293760 | tf_op jit(solution)/shard_map/all_gather | solution.py:144
  242.7 5.0 copy-start.15
  242.7 27.4 %all-to-all-start = ((bf16[4,224,1024]{2,1,0:T(8,128)(2,1)}), bf16[4,224,1024]{2,1,0:T(8,128)(2,1)S(1)}, u32[]{:S(2)}, u32[]{:S(2)}) async-start(bf16[4,224,1024]{2,1,0:T(8,128)(2,1)} %stack.2), calls=%async_computation | async-start | bytes 3670016 | tf_op jit(solution)/shard_map/all_to_all | solution.py:146
  247.7 282.0 %reduce-scatter.2.cloned.1.call-start = ((), (), s32[]{:S(2)}) async-start(), calls=%async_computation.7 | async-start | bytes 4259840 | tf_op jit(solution)/shard_map/reduce_scatter | solution.py:203
  315.7 29.6 %copy-start = (bf16[256,4096]{0,1:T(8,128)(2,1)S(1)}, bf16[256,4096]{0,1:T(8,128)(2,1)}, u32[]{:S(2)}) copy-start(bf16[256,4096]{0,1:T(8,128)(2,1)} %all-gather.10.cloned.1.call-done) | copy-start | bytes 6291460
  384.5 1.4 copy-start.10
  384.5 1.4 copy-start.12
  384.6 4.3 copy-start.4
  384.6 4.3 copy-start.5
  384.6 145.1 %copy-start.8 = (bf16[256,64]{0,1:T(8,128)(2,1)S(1)}, bf16[256,64]{0,1:T(8,128)(2,1)}, u32[]{:S(2)}) copy-start(bf16[256,64]{0,1:T(8,128)(2,1)} %fusion.30) | copy-start | bytes 98308
  (3 other events, 2.9 us)
Sparse Core Ops, SparseCore 0:
  10.8 80.2 all-gather.5
  163.7 73.6 all-gather.7
  240.7 74.9 all-gather.9
  317.4 27.8 all-gather.11
  346.9 31.1 all-gather.13
  384.7 144.9 reduce-scatter.1
